TPU v7x, 32 devices: a whole 2x2x4 slice. The times are simulated.
32 devices in a mesh: dp: 8 (over z, x), tensor: 4 (over y, core).
Axes of the slice: x: 2, y: 2, z: 4, core: 2. Of those that a mesh axis runs over, the one named last changes fastest.
Arguments:
- hidden_in: bfloat16 [10240, 2048], P(('dp', 'tensor')), may hold values from -6 to 6
- skip_mask: int32 [10240], P(('dp', 'tensor')), may hold values 0 or 1
- parents: int32 [8, 10], P('dp'), may hold values from 0 to 5, as said below
- attention_gain: bfloat16 [2048], P('dp'), may hold values from 0.099609375 to 1.8984375
- query_weight: bfloat16 [2048, 2048], P('dp', 'tensor'), may hold values from -0.25 to 0.25
- key_weight: bfloat16 [2048, 512], P('dp', 'tensor'), may hold values from -0.125 to 0.125
- value_weight: bfloat16 [2048, 512], P('dp', 'tensor'), may hold values from -0.125 to 0.125
- output_weight: bfloat16 [2048, 2048], P('dp', 'tensor'), may hold values from -0.5 to 0.5
- feedforward_gain: bfloat16 [2048], P('dp'), may hold values from 0.099609375 to 1.8984375
- gate_weight: bfloat16 [2048, 5632], P('dp', 'tensor'), may hold values from -0.125 to 0.125
- up_weight: bfloat16 [2048, 5632], P('dp', 'tensor'), may hold values from -0.125 to 0.125
- down_weight: bfloat16 [2048, 5632], P('dp', 'tensor'), may hold values from -0.15625 to 0.15625
- grad_out: bfloat16 [10240, 2048], P(('dp', 'tensor')), may hold values from -6 to 6
Outputs:
- layer_out: bfloat16 [10240, 2048], P(('dp', 'tensor'))
- input_grad: float32 [10240, 2048], P(('dp', 'tensor'))
- grad_attention_gain: float32 [2048], P('dp')
- grad_query_weight: float32 [2048, 2048], P('dp', 'tensor')
- grad_key_weight: float32 [2048, 512], P('dp', 'tensor')
- grad_value_weight: float32 [2048, 512], P('dp', 'tensor')
- grad_output_weight: float32 [2048, 2048], P('dp', 'tensor')
- grad_feedforward_gain: float32 [2048], P('dp')
- grad_gate_weight: float32 [2048, 5632], P('dp', 'tensor')
- grad_up_weight: float32 [2048, 5632], P('dp', 'tensor')
- grad_down_weight: float32 [2048, 5632], P('dp', 'tensor')
Inputs may be any that keep to these rules, and one draw needn't show every extreme that they name: `parents`: in every tree, blocks 0 to 3 form a chain (block 0 is its own parent, block b has parent b - 1); the next 2 blocks have parent 4 - 1; each of the last 4 blocks has one of those 2 blocks as parent, and each of those 2 blocks is parent of exactly 2 of the last 4 blocks.
All inputs are finite; a program needn't handle non-finite values. No bound on the sum of `skip_mask` on one device may be relied on, other than what follows from the above.
Results may differ from a plain program's by a relative error of at most 0.023.
Values may be sent and summed in bfloat16 or wider, within the bound.
No kernel may reach another device: no remote copies, remote signals or barrier semaphores. Data moves between devices by JAX's collectives and lax.ppermute only.
A program may use at most 192 MiB of HBM per device.

v0:
```python
import math
import jax
import jax.numpy as jnp
from jax import lax
from jax.sharding import PartitionSpec as P

HD = 128
epsilon = 1e-05
masked_score = -1000000000.0


def tree_layout(parent_ids):
    count = parent_ids.shape[0]
    blocks = jnp.arange(count, dtype=jnp.int32)
    ancestor = blocks[:, None] == blocks[None, :]
    current = blocks
    for sweep in range(count):
        current = jnp.sum(
            jnp.where(blocks[None, :] == current[:, None], parent_ids[None, :], 0), axis=1
        )
        ancestor = ancestor | (blocks[None, :] == current[:, None])
    depth = jnp.sum(ancestor.astype(jnp.int32), axis=1) - 1
    return (ancestor, depth)


def tree_tables(ancestor, depth, block_len, head_size):
    count = depth.shape[0]
    length = count * block_len
    visible = jnp.broadcast_to(
        ancestor[:, None, :, None], (count, block_len, count, block_len)
    ).reshape(length, length)
    places = jnp.arange(length, dtype=jnp.int32)
    block_of = places // block_len
    later = (block_of[:, None] == block_of[None, :]) & (places[None, :] > places[:, None])
    allowed = visible & jnp.logical_not(later)
    block_ids = jnp.arange(count, dtype=jnp.int32)
    row_depth = jnp.sum(
        jnp.where(block_of[:, None] == block_ids[None, :], depth[None, :], 0), axis=1
    )
    position = (row_depth * block_len + places % block_len).astype(jnp.float32)
    half_size = head_size // 2
    freqs = jnp.exp(
        jnp.arange(half_size, dtype=jnp.float32) * (-2.0 * math.log(10000.0) / head_size)
    )
    angles = position[:, None] * freqs[None, :]
    cosine = jnp.concatenate([jnp.cos(angles), jnp.cos(angles)], axis=1)[:, None, :]
    sine = jnp.concatenate([jnp.sin(angles), jnp.sin(angles)], axis=1)[:, None, :]
    return (allowed, cosine, sine)


def rotate(values_in, cosine, sine):
    half_size = values_in.shape[-1] // 2
    turned = jnp.concatenate([-values_in[..., half_size:], values_in[..., :half_size]], axis=-1)
    return values_in * cosine + turned * sine


def rotate_back(grads_in, cosine, sine):
    half_size = grads_in.shape[-1] // 2
    scaled = grads_in * sine
    return grads_in * cosine + jnp.concatenate(
        [scaled[..., half_size:], -scaled[..., :half_size]], axis=-1
    )


def rms_scale(values_in):
    return lax.rsqrt(jnp.mean(values_in * values_in, axis=-1, keepdims=True) + epsilon)


def body(
    hidden_in,
    skip_mask,
    parents,
    attention_gain,
    query_weight,
    key_weight,
    value_weight,
    output_weight,
    feedforward_gain,
    gate_weight,
    up_weight,
    down_weight,
    grad_out,
):
    local_rows = hidden_in.shape[0]
    length = local_rows * lax.axis_size("tensor")
    parent_ids = parents[0]
    block_len = length // parent_ids.shape[0]
    ancestor, depth = tree_layout(parent_ids)
    allowed, cosine, sine = tree_tables(ancestor, depth, block_len, HD)
    keep = (1 - skip_mask).astype(jnp.float32)[:, None]

    def attention_weights():
        return (
            lax.all_gather(attention_gain, "dp", axis=0, tiled=True),
            lax.all_gather(query_weight, "dp", axis=0, tiled=True),
            lax.all_gather(key_weight, "dp", axis=0, tiled=True),
            lax.all_gather(value_weight, "dp", axis=0, tiled=True),
            lax.all_gather(output_weight, "dp", axis=0, tiled=True),
        )

    def feedforward_weights():
        return (
            lax.all_gather(feedforward_gain, "dp", axis=0, tiled=True),
            lax.all_gather(gate_weight, "dp", axis=0, tiled=True),
            lax.all_gather(up_weight, "dp", axis=0, tiled=True),
            lax.all_gather(down_weight, "dp", axis=0, tiled=True),
        )

    def gain_total(partial_sum):
        return lax.psum(partial_sum, "tensor")

    gain_one, weight_query, weight_key, weight_value, weight_output = attention_weights()
    inputs = hidden_in.astype(jnp.float32)
    scale_one = rms_scale(inputs)
    unit_one = inputs * scale_one
    normed = (unit_one * gain_one.astype(jnp.float32)).astype(jnp.bfloat16)
    normed_all = lax.all_gather(normed, "tensor", axis=0, tiled=True)
    heads_dev = weight_query.shape[1] // HD
    kv_dev = weight_key.shape[1] // HD
    group = heads_dev // kv_dev
    scale = HD ** (-0.5)
    half_len = length // 2
    items = heads_dev * 2
    query_raw = jnp.dot(normed_all, weight_query, preferred_element_type=jnp.float32).reshape(
        length, heads_dev, HD
    )
    key_raw = jnp.dot(normed_all, weight_key, preferred_element_type=jnp.float32).reshape(
        length, kv_dev, HD
    )
    values_all = jnp.dot(normed_all, weight_value, preferred_element_type=jnp.float32).astype(
        jnp.bfloat16
    )
    queries = rotate(query_raw, cosine, sine).astype(jnp.bfloat16)
    keys_rot = rotate(key_raw, cosine, sine).astype(jnp.bfloat16)
    query_items = queries.transpose(1, 0, 2).reshape(items, half_len, HD)
    key_heads = keys_rot.transpose(1, 0, 2)
    value_heads = values_all.reshape(length, kv_dev, HD).transpose(1, 0, 2)
    item_ids = jnp.arange(items, dtype=jnp.int32)

    def item_scores(query_block, item):
        kv_index = item // 2 // group
        key_block = lax.dynamic_index_in_dim(key_heads, kv_index, 0, keepdims=False)
        value_block = lax.dynamic_index_in_dim(value_heads, kv_index, 0, keepdims=False)
        mask_rows = lax.dynamic_slice_in_dim(allowed, item % 2 * half_len, half_len, 0)
        scores = (
            jnp.einsum("rd,md->rm", query_block, key_block, preferred_element_type=jnp.float32)
            * scale
        )
        return (jnp.where(mask_rows, scores, masked_score), key_block, value_block)

    def attend_item(operands):
        query_block, item = operands
        scores, key_block, value_block = item_scores(query_block, item)
        top = jnp.max(scores, axis=-1, keepdims=True)
        weights_raw = jnp.exp(scores - top)
        total = jnp.sum(weights_raw, axis=-1, keepdims=True)
        probs = weights_raw / total
        mixed_block = jnp.dot(
            probs.astype(jnp.bfloat16), value_block, preferred_element_type=jnp.float32
        ).astype(jnp.bfloat16)
        return (mixed_block, (top + jnp.log(total))[:, 0])

    mixed_items, log_totals = lax.map(attend_item, (query_items, item_ids))
    mixed = (
        mixed_items.reshape(heads_dev, length, HD)
        .transpose(1, 0, 2)
        .reshape(length, heads_dev * HD)
    )
    attended = lax.psum_scatter(
        jnp.einsum("lc,dc->ld", mixed, weight_output, preferred_element_type=jnp.float32),
        "tensor",
        scatter_dimension=0,
        tiled=True,
    )
    middle = inputs + keep * attended
    gain_two, weight_gate, weight_up, weight_down = feedforward_weights()
    scale_two = rms_scale(middle)
    unit_two = middle * scale_two
    normed_ff = (unit_two * gain_two.astype(jnp.float32)).astype(jnp.bfloat16)
    normed_ff_all = lax.all_gather(normed_ff, "tensor", axis=0, tiled=True)
    gate = jnp.dot(normed_ff_all, weight_gate, preferred_element_type=jnp.float32)
    upward = jnp.dot(normed_ff_all, weight_up, preferred_element_type=jnp.float32)
    sigma = jax.nn.sigmoid(gate)
    active = gate * sigma
    hidden_ff = (active * upward).astype(jnp.bfloat16)
    branch = lax.psum_scatter(
        jnp.einsum("lf,df->ld", hidden_ff, weight_down, preferred_element_type=jnp.float32).astype(
            jnp.bfloat16
        ),
        "tensor",
        scatter_dimension=0,
        tiled=True,
    ).astype(jnp.float32)
    layer_out = (middle + keep * branch).astype(jnp.bfloat16)
    cotangent = grad_out.astype(jnp.float32)
    gain_two, weight_gate, weight_up, weight_down = feedforward_weights()
    branch_grad = (keep * cotangent).astype(jnp.bfloat16)
    branch_grad_all = lax.all_gather(branch_grad, "tensor", axis=0, tiled=True)
    hidden_grad = jnp.dot(branch_grad_all, weight_down, preferred_element_type=jnp.float32)
    grad_down = jnp.einsum(
        "ld,lf->df", branch_grad_all, hidden_ff, preferred_element_type=jnp.float32
    )
    gate_grad = (hidden_grad * upward * sigma * (1.0 + gate * (1.0 - sigma))).astype(jnp.bfloat16)
    up_grad = (hidden_grad * active).astype(jnp.bfloat16)
    grad_gate = jnp.einsum(
        "ld,lf->df", normed_ff_all, gate_grad, preferred_element_type=jnp.float32
    )
    grad_up = jnp.einsum("ld,lf->df", normed_ff_all, up_grad, preferred_element_type=jnp.float32)
    gate_part = jnp.einsum("lf,df->ld", gate_grad, weight_gate, preferred_element_type=jnp.float32)
    up_part = jnp.einsum("lf,df->ld", up_grad, weight_up, preferred_element_type=jnp.float32)
    normed_ff_grad = lax.psum_scatter(
        gate_part + up_part, "tensor", scatter_dimension=0, tiled=True
    )
    grad_gain_two = jnp.sum(normed_ff_grad * unit_two, axis=0)
    scaled_two = normed_ff_grad * gain_two.astype(jnp.float32)
    middle_grad = cotangent + scale_two * (
        scaled_two - unit_two * jnp.mean(scaled_two * unit_two, axis=-1, keepdims=True)
    )
    feedforward_grads = (
        lax.psum_scatter(
            gain_total(grad_gain_two).astype(jnp.bfloat16), "dp", scatter_dimension=0, tiled=True
        ).astype(jnp.float32),
        lax.psum_scatter(
            grad_gate.astype(jnp.bfloat16), "dp", scatter_dimension=0, tiled=True
        ).astype(jnp.float32),
        lax.psum_scatter(
            grad_up.astype(jnp.bfloat16), "dp", scatter_dimension=0, tiled=True
        ).astype(jnp.float32),
        lax.psum_scatter(
            grad_down.astype(jnp.bfloat16), "dp", scatter_dimension=0, tiled=True
        ).astype(jnp.float32),
    )
    gain_one, weight_query, weight_key, weight_value, weight_output = attention_weights()
    attended_grad = (keep * middle_grad).astype(jnp.bfloat16)
    attended_grad_all = lax.all_gather(attended_grad, "tensor", axis=0, tiled=True)
    mixed_grad = jnp.dot(
        attended_grad_all, weight_output, preferred_element_type=jnp.float32
    ).astype(jnp.bfloat16)
    grad_output = jnp.einsum(
        "ld,lc->dc", attended_grad_all, mixed, preferred_element_type=jnp.float32
    )
    mixed_grad_items = (
        mixed_grad.reshape(length, heads_dev, HD).transpose(1, 0, 2).reshape(items, half_len, HD)
    )

    def back_item(carry, operands):
        key_acc, value_acc = carry
        query_block, grad_block, log_total, item = operands
        scores, key_block, value_block = item_scores(query_block, item)
        probs = jnp.exp(scores - log_total[:, None])
        prob_grad = jnp.einsum(
            "rd,md->rm", grad_block, value_block, preferred_element_type=jnp.float32
        )
        score_grad = (
            probs * (prob_grad - jnp.sum(prob_grad * probs, axis=-1, keepdims=True))
        ).astype(jnp.bfloat16)
        query_grad = jnp.dot(score_grad, key_block, preferred_element_type=jnp.float32) * scale
        key_part = (
            jnp.einsum("rm,rd->md", score_grad, query_block, preferred_element_type=jnp.float32)
            * scale
        )
        value_part = jnp.einsum(
            "rm,rd->md", probs.astype(jnp.bfloat16), grad_block, preferred_element_type=jnp.float32
        )
        kv_index = item // 2 // group
        key_acc = key_acc.at[kv_index].add(key_part)
        value_acc = value_acc.at[kv_index].add(value_part)
        return ((key_acc, value_acc), query_grad)

    empty_heads = jnp.zeros((kv_dev, length, HD), jnp.float32)
    (key_acc, value_acc), query_grads = lax.scan(
        back_item, (empty_heads, empty_heads), (query_items, mixed_grad_items, log_totals, item_ids)
    )
    query_rot_grad = query_grads.reshape(heads_dev, length, HD).transpose(1, 0, 2)
    query_raw_grad = (
        rotate_back(query_rot_grad, cosine, sine)
        .astype(jnp.bfloat16)
        .reshape(length, heads_dev * HD)
    )
    key_raw_grad = (
        rotate_back(key_acc.transpose(1, 0, 2), cosine, sine)
        .astype(jnp.bfloat16)
        .reshape(length, kv_dev * HD)
    )
    value_grad = value_acc.transpose(1, 0, 2).astype(jnp.bfloat16).reshape(length, kv_dev * HD)
    grad_query = jnp.einsum(
        "ld,lc->dc", normed_all, query_raw_grad, preferred_element_type=jnp.float32
    )
    grad_key = jnp.einsum("ld,lc->dc", normed_all, key_raw_grad, preferred_element_type=jnp.float32)
    grad_value = jnp.einsum("ld,lc->dc", normed_all, value_grad, preferred_element_type=jnp.float32)
    query_part = jnp.einsum(
        "lc,dc->ld", query_raw_grad, weight_query, preferred_element_type=jnp.float32
    )
    key_part = jnp.einsum("lc,dc->ld", key_raw_grad, weight_key, preferred_element_type=jnp.float32)
    value_part = jnp.einsum(
        "lc,dc->ld", value_grad, weight_value, preferred_element_type=jnp.float32
    )
    normed_grad = lax.psum_scatter(
        (query_part + key_part + value_part).astype(jnp.bfloat16),
        "tensor",
        scatter_dimension=0,
        tiled=True,
    ).astype(jnp.float32)
    grad_gain_one = jnp.sum(normed_grad * unit_one, axis=0)
    scaled_one = normed_grad * gain_one.astype(jnp.float32)
    input_grad = middle_grad + scale_one * (
        scaled_one - unit_one * jnp.mean(scaled_one * unit_one, axis=-1, keepdims=True)
    )
    attention_grads = (
        lax.psum_scatter(
            gain_total(grad_gain_one).astype(jnp.bfloat16), "dp", scatter_dimension=0, tiled=True
        ).astype(jnp.float32),
        lax.psum_scatter(
            grad_query.astype(jnp.bfloat16), "dp", scatter_dimension=0, tiled=True
        ).astype(jnp.float32),
        lax.psum_scatter(
            grad_key.astype(jnp.bfloat16), "dp", scatter_dimension=0, tiled=True
        ).astype(jnp.float32),
        lax.psum_scatter(
            grad_value.astype(jnp.bfloat16), "dp", scatter_dimension=0, tiled=True
        ).astype(jnp.float32),
        lax.psum_scatter(
            grad_output.astype(jnp.bfloat16), "dp", scatter_dimension=0, tiled=True
        ).astype(jnp.float32),
    )
    return (
        layer_out,
        input_grad,
        attention_grads[0],
        attention_grads[1],
        attention_grads[2],
        attention_grads[3],
        attention_grads[4],
        feedforward_grads[0],
        feedforward_grads[1],
        feedforward_grads[2],
        feedforward_grads[3],
    )


def solution(mesh):
    return jax.shard_map(
        body,
        mesh=mesh,
        in_specs=(
            P(("dp", "tensor"), None),
            P(("dp", "tensor")),
            P("dp", None),
            P("dp"),
            P("dp", "tensor"),
            P("dp", "tensor"),
            P("dp", "tensor"),
            P("dp", "tensor"),
            P("dp"),
            P("dp", "tensor"),
            P("dp", "tensor"),
            P("dp", "tensor"),
            P(("dp", "tensor"), None),
        ),
        out_specs=(
            P(("dp", "tensor"), None),
            P(("dp", "tensor"), None),
            P("dp"),
            P("dp", "tensor"),
            P("dp", "tensor"),
            P("dp", "tensor"),
            P("dp", "tensor"),
            P("dp"),
            P("dp", "tensor"),
            P("dp", "tensor"),
            P("dp", "tensor"),
        ),
        check_vma=False,
    )
```

profile of v0, /device:TPU:0, one launch (start us, length us, event | category | flops | bytes accessed | tf_op | source)
XLA Modules:
  0.0 1618.3 jit_solution(11621017453243583606)
XLA Ops:
  7.9 22.2 %all-gather = bf16[8,1,256]{2,1,0:T(2,128)(2,1)S(1)} all-gather(bf16[1,1,256]{2,1,0:T(2,128)(2,1)S(1)} %reshape.568), channel_id=1, replica_groups=mesh['dp'=8,'tensor'=4] {'dp'}, dimensions={0}, use_global_device_ids=true | all-gather | bytes 4608 | tf_op jit(solution)/shard_map/all_gather | solution.py:94
  38.9 31.5 %all_gather.51 = bf16[2048,128]{1,0:T(8,128)(2,1)S(1)} all-gather(bf16[256,128]{1,0:T(8,128)(2,1)S(1)} %copy-done.25), channel_id=1, replica_groups=mesh['dp'=8,'tensor'=4] {'dp'}, dimensions={0}, use_global_device_ids=true | all-gather | bytes 589824 | tf_op jit(solution)/shard_map/all_gather | solution.py:96
  71.2 4.3 fusion.41
  75.4 32.5 %all_gather.52 = bf16[2048,128]{1,0:T(8,128)(2,1)S(1)} all-gather(bf16[256,128]{1,0:T(8,128)(2,1)S(1)} %copy-done.26), channel_id=1, replica_groups=mesh['dp'=8,'tensor'=4] {'dp'}, dimensions={0}, use_global_device_ids=true | all-gather | bytes 589824 | tf_op jit(solution)/shard_map/all_gather | solution.py:97
  109.9 4.5 fusion.94
  114.5 12.2 all-gather.14.cloned.1.call-done
  126.7 6.2 fusion.93
  137.1 4.7 fusion.58
  141.9 72.3 %while.34 = (s32[]{:T(128)}, bf16[8,640,128]{2,1,0:T(8,128)(2,1)}, f32[8,640]{1,0:T(8,128)}, s32[8]{0:T(128)S(1)}, pred[1280,1280]{1,0:T(32,128)(4,1)}, /*index=...) while((s32[]{:T(128)}, bf16[8,640,128]{2,1,0:T(8,128)(2,1)}, ...), condition=%wide.region_16.17_spmd, body=%wide.region_13.16_spmd.sunk | while | flops 426065280 | bytes 11664684 | solution.py:163
  215.8 7.6 fusion.95
  224.1 18.1 %all-gather.1 = bf16[8,1,256]{2,1,0:T(2,128)(2,1)S(1)} all-gather(bf16[1,1,256]{2,1,0:T(2,128)(2,1)S(1)} %reshape.570), channel_id=1, replica_groups=mesh['dp'=8,'tensor'=4] {'dp'}, dimensions={0}, use_global_device_ids=true | all-gather | bytes 4608 | tf_op jit(solution)/shard_map/all_gather | solution.py:103
  242.3 65.2 %reduce-scatter.12.cloned.1.call-done = f32[320,2048]{1,0:T(8,128)} async-done(((f32[1280,2048]{1,0:T(8,128)}), f32[320,2048]{1,0:T(8,128)}) %reduce-scatter.12.cloned.1.call-update) | async-done | bytes 2621456 | tf_op jit(solution)/shard_map/reduce_scatter | solution.py:169
  307.5 4.4 multiply_reduce_fusion.3
  315.7 86.4 %all-gather.20.cloned.1.call-done = bf16[2048,1408]{1,0:T(8,128)(2,1)} async-done(((bf16[256,1408]{1,0:T(8,128)(2,1)}), bf16[2048,1408]{1,0:T(8,128)(2,1)}) %all-gather.20.cloned.1.call-update) | async-done | bytes 5767184 | tf_op jit(solution)/shard_map/all_gather | solution.py:104
  402.2 40.6 %all-gather.18.cloned.1.call-done = bf16[1280,2048]{1,0:T(8,128)(2,1)} async-done(((bf16[320,2048]{1,0:T(8,128)(2,1)}), bf16[1280,2048]{1,0:T(8,128)(2,1)}) %all-gather.18.cloned.1.call-update) | async-done | bytes 5242896 | tf_op jit(solution)/shard_map/all_gather | solution.py:180
  442.8 13.9 fusion.96
  456.7 81.0 %all-gather.22.cloned.1.call-done = bf16[2048,1408]{1,0:T(8,128)(2,1)} async-done(((bf16[256,1408]{1,0:T(8,128)(2,1)}), bf16[2048,1408]{1,0:T(8,128)(2,1)}) %all-gather.22.cloned.1.call-update) | async-done | bytes 5767184 | tf_op jit(solution)/shard_map/all_gather | solution.py:105
  537.7 13.8 fusion.97
  551.4 79.3 %all-gather.24.cloned.1.call-done = bf16[2048,1408]{1,0:T(8,128)(2,1)} async-done(((bf16[256,1408]{1,0:T(8,128)(2,1)}), bf16[2048,1408]{1,0:T(8,128)(2,1)}) %all-gather.24.cloned.1.call-update) | async-done | bytes 5767184 | tf_op jit(solution)/shard_map/all_gather | solution.py:106
  630.7 40.8 %all-gather.26.cloned.1.call-done = bf16[1280,2048]{1,0:T(8,128)(2,1)} async-done(((bf16[320,2048]{1,0:T(8,128)(2,1)}), bf16[1280,2048]{1,0:T(8,128)(2,1)}) %all-gather.26.cloned.1.call-update) | async-done | bytes 5242896 | tf_op jit(solution)/shard_map/all_gather | solution.py:198
  671.5 19.3 %multiply_convert_fusion.1 = (bf16[1280,1408]{1,0:T(8,128)(2,1)S(1)}, bf16[1280,1408]{1,0:T(8,128)(2,1)}, bf16[1280,1408]{1,0:T(8,128)(2,1)}) fusion(f32[1280,1408]{1,0:T(8,128)} %fusion.96, f32[1280,1408]{1,0:T(8,128)} %fusion.97, bf16[1280,2048]{1,0:T(8,128)(2,1)} %all-gather.26.cloned.1.call-done, bf16[2048,1408]{1,0:T(8,128)(2,1)} %all-gather.24.cloned.1.call-done), kind=kOutput, calls=%fused_computation.56 | convolution fusion | flops 7409008640 | bytes 36241408 | tf_op jit(solution)/shard_map/dot_general | solution.py:199
  690.8 15.1 fusion.98
  705.9 13.2 convolution_add_fusion
  719.1 13.3 convolution_convert_fusion.3
  732.5 72.0 %reduce-scatter.16.cloned.1.call-done = f32[320,2048]{1,0:T(8,128)} async-done(((f32[1280,2048]{1,0:T(8,128)}), f32[320,2048]{1,0:T(8,128)}) %reduce-scatter.16.cloned.1.call-update) | async-done | bytes 2621456 | tf_op jit(solution)/shard_map/reduce_scatter | solution.py:211
  807.5 50.9 %reduce-scatter.14.cloned.1.call-done = bf16[320,2048]{1,0:T(8,128)(2,1)} async-done(((bf16[1280,2048]{1,0:T(8,128)(2,1)}), bf16[320,2048]{1,0:T(8,128)(2,1)}) %reduce-scatter.14.cloned.1.call-update) | async-done | bytes 1310736 | tf_op jit(solution)/shard_map/reduce_scatter | solution.py:186
  858.5 5.1 multiply_convert_fusion.4
  863.7 13.0 convolution_convert_fusion.2
  876.8 13.5 convolution_convert_fusion.1
  893.5 13.1 convolution_convert_fusion
  908.2 5.4 convolution_convert_fusion.6
  915.2 150.3 %while.35 = (s32[]{:T(128)}, f32[1,1280,128]{2,1,0:T(8,128)}, f32[1,1280,128]{2,1,0:T(8,128)}, f32[8,640,128]{2,1,0:T(8,128)}, s32[8]{0:T(128)S(1)}, /*index=5*/...) while((s32[]{:T(128)}, f32[1,1280,128]{2,1,0:T(8,128)}, ...), condition=%wide.region_25.26_spmd.clone, body=%wide.region_22.25_spmd.clone.sunk | while | flops 1057176960 | bytes 39174844 | solution.py:271
  1068.2 5.1 convolution_convert_fusion.8
  1075.4 5.2 convolution_convert_fusion.7
  1088.8 6.9 convolution_convert_fusion.5
  1095.7 7.1 convolution_convert_fusion.4
  1104.5 5.5 fusion.99
  1110.0 8.3 add_convert_fusion
  1122.6 9.5 reduce-scatter.30.cloned.1.call-done
  1134.4 111.4 %reduce-scatter.32.cloned.1.call-done = bf16[256,1408]{1,0:T(8,128)(2,1)} async-done(((bf16[2048,1408]{1,0:T(8,128)(2,1)}), bf16[256,1408]{1,0:T(8,128)(2,1)}) %reduce-scatter.32.cloned.1.call-update) | async-done | bytes 720912 | tf_op jit(solution)/shard_map/reduce_scatter | solution.py:229
  1248.1 63.0 %reduce-scatter.22.cloned.1.call-done = bf16[256,128]{1,0:T(8,128)(2,1)} async-done(((bf16[2048,128]{1,0:T(8,128)(2,1)}), bf16[256,128]{1,0:T(8,128)(2,1)}) %reduce-scatter.22.cloned.1.call-update) | async-done | bytes 65552 | tf_op jit(solution)/shard_map/reduce_scatter | solution.py:316
  1312.6 62.6 %reduce-scatter.24.cloned.1.call-done = bf16[256,128]{1,0:T(8,128)(2,1)} async-done(((bf16[2048,128]{1,0:T(8,128)(2,1)}), bf16[256,128]{1,0:T(8,128)(2,1)}) %reduce-scatter.24.cloned.1.call-update) | async-done | bytes 65552 | tf_op jit(solution)/shard_map/reduce_scatter | solution.py:319
  1376.8 69.7 %reduce-scatter.20.cloned.1.call-done = bf16[256,512]{1,0:T(8,128)(2,1)} async-done(((bf16[2048,512]{1,0:T(8,128)(2,1)}), bf16[256,512]{1,0:T(8,128)(2,1)}) %reduce-scatter.20.cloned.1.call-update) | async-done | bytes 262160 | tf_op jit(solution)/shard_map/reduce_scatter | solution.py:313
  1448.3 69.0 %reduce-scatter.26.cloned.1.call-done = bf16[256,512]{1,0:T(8,128)(2,1)} async-done(((bf16[2048,512]{1,0:T(8,128)(2,1)}), bf16[256,512]{1,0:T(8,128)(2,1)}) %reduce-scatter.26.cloned.1.call-update) | async-done | bytes 262160 | tf_op jit(solution)/shard_map/reduce_scatter | solution.py:322
  1519.0 51.1 %reduce-scatter.18.cloned.1.call-done = bf16[320,2048]{1,0:T(8,128)(2,1)} async-done(((bf16[1280,2048]{1,0:T(8,128)(2,1)}), bf16[320,2048]{1,0:T(8,128)(2,1)}) %reduce-scatter.18.cloned.1.call-update) | async-done | bytes 1310736 | tf_op jit(solution)/shard_map/reduce_scatter | solution.py:298
  1572.9 10.2 all-reduce.2
  1583.0 21.7 %all-reduce.3 = (bf16[2048]{0:T(1024)(128)(2,1)S(1)}, bf16[2048]{0:T(1024)(128)(2,1)S(1)}) all-reduce(bf16[2048]{0:T(1024)(128)(2,1)S(1)} %get-tuple-element.495, bf16[2048]{0:T(1024)(128)(2,1)S(1)} %get-tuple-element.496), channel_id=6, replica_groups=mesh['dp'=8,'tensor'=4] {'dp'}, use_global_device_ids=true, to_apply=%region_30.31.clone | all-reduce | flops 4096 | bytes 16384
  1605.4 5.8 fusion.48
  (365 shorter events, 250.0 us)
Async XLA Ops:
  7.2 102.8 %all-gather.12.cloned.1.call-start = ((), (), s32[]{:S(2)}) async-start(), calls=%async_computation.11 | async-start | bytes 6553600 | tf_op jit(solution)/shard_map/all_gather | solution.py:117
  30.1 6.7 copy-start.38
  30.1 8.8 copy-start.25
  35.2 91.5 %all-gather.14.cloned.1.call-start = ((), (), s32[]{:S(2)}) async-start(), calls=%async_computation.12 | async-start | bytes 2359296 | tf_op jit(solution)/shard_map/all_gather | solution.py:95
  36.0 179.9 %all-gather.16.cloned.1.call-start = ((), (), s32[]{:S(2)}) async-start(), calls=%async_computation.13 | async-start | bytes 2359296 | tf_op jit(solution)/shard_map/all_gather | solution.py:98
  36.7 270.8 %reduce-scatter.12.cloned.1.call-start = ((), (), s32[]{:S(2)}) async-start(), calls=%async_computation.14 | async-start | bytes 13107200 | tf_op jit(solution)/shard_map/reduce_scatter | solution.py:169
  70.4 39.6 %copy-start.9 = (bf16[2048,128]{1,0:T(8,128)(2,1)}, bf16[2048,128]{1,0:T(8,128)(2,1)S(1)}, u32[]{:S(2)}) copy-start(bf16[2048,128]{1,0:T(8,128)(2,1)S(1)} %all_gather.51) | copy-start | bytes 1572868
  71.1 4.3 copy-start.26
  108.0 29.2 %copy-start.15 = (bf16[2048,128]{1,0:T(8,128)(2,1)}, bf16[2048,128]{1,0:T(8,128)(2,1)S(1)}, u32[]{:S(2)}) copy-start(bf16[2048,128]{1,0:T(8,128)(2,1)S(1)} %all_gather.52) | copy-start | bytes 1572868
  109.9 23.2 %copy-start.11 = (f32[1280,64]{0,1:T(8,128)}, f32[1280,64]{0,1:T(8,128)S(1)}, u32[]{:S(2)}) copy-start(f32[1280,64]{0,1:T(8,128)S(1)} %get-tuple-element.525) | copy-start | bytes 983044
  215.8 7.6 copy-start.19
  223.4 18.8 %copy-start.34 = (s32[320]{0:T(512)S(1)}, s32[320]{0:T(512)}, u32[]{:S(2)}) copy-start(s32[320]{0:T(512)} %param.22) | copy-start | bytes 3844
  223.5 178.7 %all-gather.20.cloned.1.call-start = ((), (), s32[]{:S(2)}) async-start(), calls=%async_computation.16 | async-start | bytes 6488064 | tf_op jit(solution)/shard_map/all_gather | solution.py:104
  224.0 218.8 %all-gather.18.cloned.1.call-start = ((), (), s32[]{:S(2)}) async-start(), calls=%async_computation.15 | async-start | bytes 6553600 | tf_op jit(solution)/shard_map/all_gather | solution.py:180
  242.2 616.2 %copy-start.21 = (f32[8,1,256]{2,1,0:T(1,128)}, f32[8,1,256]{2,1,0:T(1,128)S(1)}, u32[]{:S(2)}) copy-start(f32[8,1,256]{2,1,0:T(1,128)S(1)} %convert_element_type.220) | copy-start | bytes 24580
  311.9 546.6 %copy-start.1 = (f32[320,2048]{1,0:T(8,128)}, f32[320,2048]{1,0:T(8,128)S(1)}, u32[]{:S(2)}) copy-start(f32[320,2048]{1,0:T(8,128)S(1)} %get-tuple-element.500) | copy-start | bytes 7864324
  311.9 546.6 %copy-start.27 = (f32[320]{0:T(512)}, f32[320]{0:T(512)S(1)}, u32[]{:S(2)}) copy-start(f32[320]{0:T(512)S(1)} %add_rsqrt_fusion) | copy-start | bytes 3844
  313.4 224.2 %all-gather.22.cloned.1.call-start = ((), (), s32[]{:S(2)}) async-start(), calls=%async_computation.17 | async-start | bytes 6488064 | tf_op jit(solution)/shard_map/all_gather | solution.py:105
  314.2 316.5 %all-gather.24.cloned.1.call-start = ((), (), s32[]{:S(2)}) async-start(), calls=%async_computation.18 | async-start | bytes 6488064 | tf_op jit(solution)/shard_map/all_gather | solution.py:106
  314.9 356.6 %all-gather.26.cloned.1.call-start = ((), (), s32[]{:S(2)}) async-start(), calls=%async_computation.20 | async-start | bytes 6553600 | tf_op jit(solution)/shard_map/all_gather | solution.py:198
  315.7 488.8 %reduce-scatter.16.cloned.1.call-start = ((), (), s32[]{:S(2)}) async-start(), calls=%async_computation.21 | async-start | bytes 13107200 | tf_op jit(solution)/shard_map/reduce_scatter | solution.py:211
  690.8 15.1 copy-start.41
  690.8 15.1 copy-start.35
  719.1 139.4 %reduce-scatter.14.cloned.1.call-start = ((), (), s32[]{:S(2)}) async-start(), calls=%async_computation.19 | async-start | bytes 6553600 | tf_op jit(solution)/shard_map/reduce_scatter | solution.py:186
  732.5 174.2 %all-gather.28.cloned.1.call-start = ((), (), s32[]{:S(2)}) async-start(), calls=%async_computation.22 | async-start | bytes 6553600 | tf_op jit(solution)/shard_map/all_gather | solution.py:235
  807.5 56.1 %copy-start.32 = (f32[320]{0:T(512)}, f32[320]{0:T(512)S(1)}, u32[]{:S(2)}) copy-start(f32[320]{0:T(512)S(1)} %broadcast_multiply_fusion.1) | copy-start | bytes 3844
  863.6 256.6 %reduce-scatter.28.cloned.1.call-start = ((), (), s32[]{:S(2)}) async-start(), calls=%async_computation.28 | async-start | bytes 6488064 | tf_op jit(solution)/shard_map/reduce_scatter | solution.py:223
  876.7 255.3 %reduce-scatter.30.cloned.1.call-start = ((), (), s32[]{:S(2)}) async-start(), calls=%async_computation.29 | async-start | bytes 6488064 | tf_op jit(solution)/shard_map/reduce_scatter | solution.py:226
  890.3 355.5 %reduce-scatter.32.cloned.1.call-start = ((), (), s32[]{:S(2)}) async-start(), calls=%async_computation.30 | async-start | bytes 6488064 | tf_op jit(solution)/shard_map/reduce_scatter | solution.py:229
  906.6 404.5 %reduce-scatter.22.cloned.1.call-start = ((), (), s32[]{:S(2)}) async-start(), calls=%async_computation.25 | async-start | bytes 589824 | tf_op jit(solution)/shard_map/reduce_scatter | solution.py:316
  1068.2 5.1 copy-start.17
  1068.2 5.1 copy-start.14
  1075.4 299.9 %reduce-scatter.24.cloned.1.call-start = ((), (), s32[]{:S(2)}) async-start(), calls=%async_computation.26 | async-start | bytes 589824 | tf_op jit(solution)/shard_map/reduce_scatter | solution.py:319
  1080.6 3.3 copy-start.13
  1083.9 362.6 %reduce-scatter.20.cloned.1.call-start = ((), (), s32[]{:S(2)}) async-start(), calls=%async_computation.24 | async-start | bytes 2359296 | tf_op jit(solution)/shard_map/reduce_scatter | solution.py:313
  1088.8 7.0 copy-start.20
  1095.7 7.2 copy-start.10
  1095.7 7.2 copy-start.18
  1095.7 421.6 %reduce-scatter.26.cloned.1.call-start = ((), (), s32[]{:S(2)}) async-start(), calls=%async_computation.27 | async-start | bytes 2359296 | tf_op jit(solution)/shard_map/reduce_scatter | solution.py:322
  1102.8 467.3 %reduce-scatter.18.cloned.1.call-start = ((), (), s32[]{:S(2)}) async-start(), calls=%async_computation.23 | async-start | bytes 6553600 | tf_op jit(solution)/shard_map/reduce_scatter | solution.py:298
  1104.5 5.5 copy-start.16
  1122.6 447.6 %copy-start.24 = (f32[8,1,256]{2,1,0:T(1,128)S(1)}, f32[8,1,256]{2,1,0:T(1,128)}, u32[]{:S(2)}) copy-start(f32[8,1,256]{2,1,0:T(1,128)} %copy-done.23) | copy-start | bytes 24580
  1122.6 447.6 %copy-start.31 = (f32[320]{0:T(512)S(1)}, f32[320]{0:T(512)}, u32[]{:S(2)}) copy-start(f32[320]{0:T(512)} %copy-done.30) | copy-start | bytes 3844
  1248.1 324.8 %copy-start.29 = (f32[2048]{0:T(1024)S(1)}, f32[2048]{0:T(1024)}, u32[]{:S(2)}) copy-start(f32[2048]{0:T(1024)} %get-tuple-element.453) | copy-start | bytes 24580
  1248.1 357.3 %copy-start.2 = (f32[320,2048]{1,0:T(8,128)S(1)}, f32[320,2048]{1,0:T(8,128)}, u32[]{:S(2)}) copy-start(f32[320,2048]{1,0:T(8,128)} %copy-done.1) | copy-start | bytes 7864324
  1248.1 357.3 %copy-start.22 = (f32[8,1,256]{2,1,0:T(1,128)S(1)}, f32[8,1,256]{2,1,0:T(1,128)}, u32[]{:S(2)}) copy-start(f32[8,1,256]{2,1,0:T(1,128)} %copy-done.21) | copy-start | bytes 24580
  1248.1 357.3 %copy-start.28 = (f32[320]{0:T(512)S(1)}, f32[320]{0:T(512)}, u32[]{:S(2)}) copy-start(f32[320]{0:T(512)} %copy-done.27) | copy-start | bytes 3844
  1248.1 357.3 %copy-start.33 = (f32[320]{0:T(512)S(1)}, f32[320]{0:T(512)}, u32[]{:S(2)}) copy-start(f32[320]{0:T(512)} %copy-done.32) | copy-start | bytes 3844
  (35 other events, 63.0 us)
Sparse Core Ops, SparseCore 0:
  35.3 37.8 all-gather.11
  75.4 51.2 all-gather.13
  128.8 47.7 all-gather.15
  223.6 83.8 reduce-scatter.11
  309.5 92.6 all-gather.19
  404.2 38.6 all-gather.17
  445.0 92.6 all-gather.21
  539.8 90.8 all-gather.23
  632.8 38.6 all-gather.25
  719.2 85.2 reduce-scatter.15
  807.1 51.3 reduce-scatter.13
  863.8 40.4 all-gather.27
  908.3 109.9 reduce-scatter.27
  1022.3 109.7 reduce-scatter.29
  1136.0 109.7 reduce-scatter.31
  1249.3 61.7 reduce-scatter.21
  1314.3 60.9 reduce-scatter.23
  1379.6 66.7 reduce-scatter.19
  1450.4 66.7 reduce-scatter.25
  1519.8 50.3 reduce-scatter.17
where the time goes:
time: 1630 us; the launch traced here: 1620 us
  waiting for transfers between devices  969 us (59%)
  matrix products  330 us (20%)
  blocking collectives  136 us (8%)
  other arithmetic  76.7 us (5%)
  local copies, waits for them, and re-layouts  52.4 us (3%)
  loops' own time  37.5 us (2%)
    reduce_scatter x1, waiting for transfers between devices, body(): lax.psum_scatter(grad_down.astype(jnp.bfloat16), 'dp', scatter_dimension=...  111 us
    all_gather x1, waiting for transfers between devices, feedforward_weights(): lax.all_gather(gate_weight, 'dp', axis=0, tiled=True)  86.4 us
    all_gather x1, waiting for transfers between devices, feedforward_weights(): lax.all_gather(up_weight, 'dp', axis=0, tiled=True)  81 us
    all_gather x1, waiting for transfers between devices, feedforward_weights(): lax.all_gather(down_weight, 'dp', axis=0, tiled=True)  79.3 us
    reduce_scatter x1, waiting for transfers between devices, body(): lax.psum_scatter(gate_part + up_part, 'tensor', scatter_dimension=0, tile...  72 us
    reduce_scatter x1, waiting for transfers between devices, body(): lax.psum_scatter(grad_query.astype(jnp.bfloat16), 'dp', scatter_dimension...  69.7 us
    reduce_scatter x1, waiting for transfers between devices, body(): lax.psum_scatter(grad_output.astype(jnp.bfloat16), 'dp', scatter_dimensio...  69 us
    reduce_scatter x1, waiting for transfers between devices, body(): lax.psum_scatter(jnp.einsum('lc,dc->ld', mixed, weight_output, preferred_...  65.2 us
  transfers between devices with their start and end apart: 20, of which 16 were waited for; matrix products, arithmetic and copies ran while one was open for 23% of the time, Pallas kernels for 0%

commit v1 on v0

--- a/solution.py
+++ b/solution.py
@@ -7,6 +7,28 @@
 HD = 128
 epsilon = 1e-05
 masked_score = -1000000000.0
+
+
+def in_order(pieces, dim):
+    pieces = jnp.moveaxis(pieces, 0, dim)
+    lengths = pieces.shape
+    return pieces.reshape(*lengths[:dim], lengths[dim] * lengths[dim + 1], *lengths[dim + 2 :])
+
+
+def collect(shard, axis, dim):
+    size = lax.axis_size(axis)
+    pairs = [(i, (i + 1) % size) for i in range(size)]
+    back = [(b, a) for a, b in pairs]
+    lower, upper = ([], [])
+    for hop in range(size - 1):
+        if hop % 2 == 0:
+            lower.append(lax.ppermute(lower[-1] if lower else shard, axis, pairs))
+        else:
+            upper.append(lax.ppermute(upper[-1] if upper else shard, axis, back))
+    blocks = jnp.stack([*lower[::-1], shard, *upper])
+    shift = lax.axis_index(axis) - len(lower)
+    blocks = blocks[(jnp.arange(size) - shift) % size]
+    return in_order(blocks, dim)
 
 
 def tree_layout(parent_ids):
@@ -102,7 +124,7 @@
         return (
             lax.all_gather(feedforward_gain, "dp", axis=0, tiled=True),
             lax.all_gather(gate_weight, "dp", axis=0, tiled=True),
-            lax.all_gather(up_weight, "dp", axis=0, tiled=True),
+            collect(up_weight, "dp", 0),
             lax.all_gather(down_weight, "dp", axis=0, tiled=True),
         )
 

time: 1630 us -> 1630 us (level)
  waiting for transfers between devices: 969 us -> 893 us
  starting transfers between devices: 0.81 us -> 60.2 us
  local copies, waits for them, and re-layouts: 52.4 us -> 73.7 us
    ppermute x0 -> x7, waiting for transfers between devices: none -> 105 us  [the longest x4 102 us: collect(): lower.append(lax.ppermute(lower[-1] if lower else shard, axis, pairs))]
    all_gather x1, waiting for transfers between devices: 86.4 us -> 0.01 us  [feedforward_weights(): lax.all_gather(gate_weight, 'dp', axis=0, tiled=True)]
    all_gather x1 -> x0, waiting for transfers between devices: 81 us -> none  [feedforward_weights(): lax.all_gather(up_weight, 'dp', axis=0, tiled=True)]
    ppermute x0 -> x7, starting transfers between devices: none -> 59.4 us  [the longest x3 52.9 us: collect(): upper.append(lax.ppermute(upper[-1] if upper else shard, axis, back))]
  transfers between devices with their start and end apart: 20 -> 26, of which waited for: 16 -> 19; matrix products, arithmetic and copies ran while one was open for 23% -> 23% of each run, Pallas kernels for 0% -> 0%
where the time goes in v1:
time: 1630 us; the launch traced here: 1620 us
  waiting for transfers between devices  893 us (55%)
  matrix products  326 us (20%)
  blocking collectives  136 us (8%)
  other arithmetic  76.5 us (5%)
  local copies, waits for them, and re-layouts  73.7 us (5%)
  starting transfers between devices  60.2 us (4%)
  loops' own time  37.5 us (2%)
    reduce_scatter x1, waiting for transfers between devices, body(): lax.psum_scatter(grad_down.astype(jnp.bfloat16), 'dp', scatter_dimension=...  111 us
    ppermute x4, waiting for transfers between devices, collect(): lower.append(lax.ppermute(lower[-1] if lower else shard, axis, pairs))  102 us
    all_gather x1, waiting for transfers between devices, feedforward_weights(): lax.all_gather(down_weight, 'dp', axis=0, tiled=True)  81.1 us
    reduce_scatter x1, waiting for transfers between devices, body(): lax.psum_scatter(gate_part + up_part, 'tensor', scatter_dimension=0, tile...  72 us
    reduce_scatter x1, waiting for transfers between devices, body(): lax.psum_scatter(grad_query.astype(jnp.bfloat16), 'dp', scatter_dimension...  69.7 us
    reduce_scatter x1, waiting for transfers between devices, body(): lax.psum_scatter(grad_output.astype(jnp.bfloat16), 'dp', scatter_dimensio...  68.7 us
    reduce_scatter x1, waiting for transfers between devices, body(): lax.psum_scatter(jnp.einsum('lc,dc->ld', mixed, weight_output, preferred_...  65.2 us
    reduce_scatter x1, waiting for transfers between devices, body(): lax.psum_scatter(grad_key.astype(jnp.bfloat16), 'dp', scatter_dimension=0...  63 us
  transfers between devices with their start and end apart: 26, of which 19 were waited for; matrix products, arithmetic and copies ran while one was open for 23% of the time, Pallas kernels for 0%

profile of v1, /device:TPU:0, one launch (start us, length us, event | category | flops | bytes accessed | tf_op | source)
XLA Modules:
  0.0 1618.9 jit_solution(5125434262380084777)
XLA Ops:
  7.9 22.2 %all-gather = bf16[8,1,256]{2,1,0:T(2,128)(2,1)S(1)} all-gather(bf16[1,1,256]{2,1,0:T(2,128)(2,1)S(1)} %reshape.630), channel_id=1, replica_groups=mesh['dp'=8,'tensor'=4] {'dp'}, dimensions={0}, use_global_device_ids=true | all-gather | bytes 4608 | tf_op jit(solution)/shard_map/all_gather | solution.py:116
  38.9 31.5 %all_gather.47 = bf16[2048,128]{1,0:T(8,128)(2,1)S(1)} all-gather(bf16[256,128]{1,0:T(8,128)(2,1)S(1)} %copy-done.26), channel_id=1, replica_groups=mesh['dp'=8,'tensor'=4] {'dp'}, dimensions={0}, use_global_device_ids=true | all-gather | bytes 589824 | tf_op jit(solution)/shard_map/all_gather | solution.py:118
  75.4 32.8 %all_gather.48 = bf16[2048,128]{1,0:T(8,128)(2,1)S(1)} all-gather(bf16[256,128]{1,0:T(8,128)(2,1)S(1)} %copy-done.27), channel_id=1, replica_groups=mesh['dp'=8,'tensor'=4] {'dp'}, dimensions={0}, use_global_device_ids=true | all-gather | bytes 589824 | tf_op jit(solution)/shard_map/all_gather | solution.py:119
  114.7 12.0 all-gather.13.cloned.1.call-done
  126.7 6.2 fusion.95
  141.9 72.3 %while.34 = (s32[]{:T(128)}, bf16[8,640,128]{2,1,0:T(8,128)(2,1)}, f32[8,640]{1,0:T(8,128)}, s32[8]{0:T(128)S(1)}, pred[1280,1280]{1,0:T(32,128)(4,1)}, /*index=...) while((s32[]{:T(128)}, bf16[8,640,128]{2,1,0:T(8,128)(2,1)}, ...), condition=%wide.region_16.17_spmd, body=%wide.region_13.16_spmd.sunk | while | flops 426065280 | bytes 11664684 | solution.py:185
  215.8 7.6 fusion.97
  224.1 18.1 %all-gather.1 = bf16[8,1,256]{2,1,0:T(2,128)(2,1)S(1)} all-gather(bf16[1,1,256]{2,1,0:T(2,128)(2,1)S(1)} %reshape.632), channel_id=1, replica_groups=mesh['dp'=8,'tensor'=4] {'dp'}, dimensions={0}, use_global_device_ids=true | all-gather | bytes 4608 | tf_op jit(solution)/shard_map/all_gather | solution.py:125
  242.3 65.2 %reduce-scatter.12.cloned.1.call-done = f32[320,2048]{1,0:T(8,128)} async-done(((f32[1280,2048]{1,0:T(8,128)}), f32[320,2048]{1,0:T(8,128)}) %reduce-scatter.12.cloned.1.call-update) | async-done | bytes 2621456 | tf_op jit(solution)/shard_map/reduce_scatter | solution.py:191
  315.6 31.5 %collective-permute-done = bf16[256,1408]{1,0:T(8,128)(2,1)} collective-permute-done((bf16[256,1408]{1,0:T(8,128)(2,1)S(1)}, bf16[256,1408]{1,0:T(8,128)(2,1)}, u32[]{:S(2)}, u32[]{:S(2)}) %collective-permute-start) | collective-permute-done | bytes 720928 | tf_op jit(solution)/shard_map/ppermute | solution.py:25
  351.9 37.7 %collective-permute-done.1 = bf16[256,1408]{1,0:T(8,128)(2,1)} collective-permute-done((bf16[256,1408]{1,0:T(8,128)(2,1)}, bf16[256,1408]{1,0:T(8,128)(2,1)}, u32[]{:S(2)}, u32[]{:S(2)}) %collective-permute-start.1) | collective-permute-done | bytes 720928 | tf_op jit(solution)/shard_map/ppermute | solution.py:25
  392.1 30.1 %collective-permute-start.5 = (bf16[256,1408]{1,0:T(8,128)(2,1)}, bf16[256,1408]{1,0:T(8,128)(2,1)}, u32[]{:S(2)}, u32[]{:S(2)}) collective-permute-start(bf16[256,1408]{1,0:T(8,128)(2,1)} %collective-permute-done.4), channel_id=1, source_target_pairs={{4,0},{8,4},{12,8},{16,12},{20,16},{24,20},{28,24},{0,28},{5,1},{9... | collective-permute-start | bytes 2162696 | tf_op jit(solution)/shard_map/ppermute | solution.py:27
  422.1 16.0 collective-permute-done.2
  443.3 18.1 %collective-permute-start.6 = (bf16[256,1408]{1,0:T(8,128)(2,1)}, bf16[256,1408]{1,0:T(8,128)(2,1)S(1)}, u32[]{:S(2)}, u32[]{:S(2)}) collective-permute-start(bf16[256,1408]{1,0:T(8,128)(2,1)} %collective-permute-done.5), channel_id=1, source_target_pairs={{4,0},{8,4},{12,8},{16,12},{20,16},{24,20},{28,24},{0,28},{5,1},{9... | collective-permute-start | bytes 2162696 | tf_op jit(solution)/shard_map/ppermute | solution.py:27
  461.4 17.2 %collective-permute-done.3 = bf16[256,1408]{1,0:T(8,128)(2,1)} collective-permute-done((bf16[256,1408]{1,0:T(8,128)(2,1)}, bf16[256,1408]{1,0:T(8,128)(2,1)}, u32[]{:S(2)}, u32[]{:S(2)}) %collective-permute-start.3) | collective-permute-done | bytes 720928 | tf_op jit(solution)/shard_map/ppermute | solution.py:25
  492.7 7.1 gather_fusion
  499.8 26.7 %all-gather.17.cloned.1.call-done = bf16[1280,2048]{1,0:T(8,128)(2,1)} async-done(((bf16[320,2048]{1,0:T(8,128)(2,1)}), bf16[1280,2048]{1,0:T(8,128)(2,1)}) %all-gather.17.cloned.1.call-update) | async-done | bytes 5242896 | tf_op jit(solution)/shard_map/all_gather | solution.py:202
  526.5 13.8 fusion.98
  540.2 81.1 %all-gather.21.cloned.1.call-done = bf16[2048,1408]{1,0:T(8,128)(2,1)} async-done(((bf16[256,1408]{1,0:T(8,128)(2,1)}), bf16[2048,1408]{1,0:T(8,128)(2,1)}) %all-gather.21.cloned.1.call-update) | async-done | bytes 5767184 | tf_op jit(solution)/shard_map/all_gather | solution.py:128
  621.3 40.8 %all-gather.23.cloned.1.call-done = bf16[1280,2048]{1,0:T(8,128)(2,1)} async-done(((bf16[320,2048]{1,0:T(8,128)(2,1)}), bf16[1280,2048]{1,0:T(8,128)(2,1)}) %all-gather.23.cloned.1.call-update) | async-done | bytes 5242896 | tf_op jit(solution)/shard_map/all_gather | solution.py:220
  662.1 13.9 fusion.99
  676.0 17.0 %multiply_convert_fusion.1 = (bf16[1280,1408]{1,0:T(8,128)(2,1)}, bf16[1280,1408]{1,0:T(8,128)(2,1)}, bf16[1280,1408]{1,0:T(8,128)(2,1)}) fusion(f32[1280,1408]{1,0:T(8,128)} %fusion.99, f32[1280,1408]{1,0:T(8,128)} %fusion.98, bf16[1280,2048]{1,0:T(8,128)(2,1)S(1)} %copy-done.36, bf16[2048,1408]{1,0:T(8,128)(2,1)} %bitcast.223), kind=kOutput, calls=%fused_computation.57 | convolution fusion | flops 7409008640 | bytes 36241408 | tf_op jit(solution)/shard_map/dot_general | solution.py:204
  692.9 14.0 fusion.100
  706.9 13.2 convolution_add_fusion
  720.2 13.3 convolution_convert_fusion.3
  733.6 72.0 %reduce-scatter.16.cloned.1.call-done = f32[320,2048]{1,0:T(8,128)} async-done(((f32[1280,2048]{1,0:T(8,128)}), f32[320,2048]{1,0:T(8,128)}) %reduce-scatter.16.cloned.1.call-update) | async-done | bytes 2621456 | tf_op jit(solution)/shard_map/reduce_scatter | solution.py:233
  808.6 50.8 %reduce-scatter.14.cloned.1.call-done = bf16[320,2048]{1,0:T(8,128)(2,1)} async-done(((bf16[1280,2048]{1,0:T(8,128)(2,1)}), bf16[320,2048]{1,0:T(8,128)(2,1)}) %reduce-scatter.14.cloned.1.call-update) | async-done | bytes 1310736 | tf_op jit(solution)/shard_map/reduce_scatter | solution.py:208
  859.4 5.1 multiply_convert_fusion.4
  864.6 13.0 convolution_convert_fusion.2
  877.7 13.5 convolution_convert_fusion.1
  894.5 13.1 convolution_convert_fusion
  909.1 5.4 convolution_convert_fusion.6
  916.2 150.1 %while.35 = (s32[]{:T(128)}, f32[1,1280,128]{2,1,0:T(8,128)}, f32[1,1280,128]{2,1,0:T(8,128)}, f32[8,640,128]{2,1,0:T(8,128)}, s32[8]{0:T(128)S(1)}, /*index=5*/...) while((s32[]{:T(128)}, f32[1,1280,128]{2,1,0:T(8,128)}, ...), condition=%wide.region_25.26_spmd.clone, body=%wide.region_22.25_spmd.clone.sunk | while | flops 1057176960 | bytes 39174844 | solution.py:293
  1076.2 5.1 convolution_convert_fusion.7
  1089.5 6.9 convolution_convert_fusion.5
  1096.5 7.1 convolution_convert_fusion.4
  1105.2 5.6 fusion.101
  1110.8 8.3 add_convert_fusion
  1123.4 9.7 reduce-scatter.30.cloned.1.call-done
  1135.4 111.4 %reduce-scatter.32.cloned.1.call-done = bf16[256,1408]{1,0:T(8,128)(2,1)} async-done(((bf16[2048,1408]{1,0:T(8,128)(2,1)}), bf16[256,1408]{1,0:T(8,128)(2,1)}) %reduce-scatter.32.cloned.1.call-update) | async-done | bytes 720912 | tf_op jit(solution)/shard_map/reduce_scatter | solution.py:251
  1249.1 63.0 %reduce-scatter.22.cloned.1.call-done = bf16[256,128]{1,0:T(8,128)(2,1)} async-done(((bf16[2048,128]{1,0:T(8,128)(2,1)}), bf16[256,128]{1,0:T(8,128)(2,1)}) %reduce-scatter.22.cloned.1.call-update) | async-done | bytes 65552 | tf_op jit(solution)/shard_map/reduce_scatter | solution.py:338
  1313.6 62.7 %reduce-scatter.24.cloned.1.call-done = bf16[256,128]{1,0:T(8,128)(2,1)} async-done(((bf16[2048,128]{1,0:T(8,128)(2,1)}), bf16[256,128]{1,0:T(8,128)(2,1)}) %reduce-scatter.24.cloned.1.call-update) | async-done | bytes 65552 | tf_op jit(solution)/shard_map/reduce_scatter | solution.py:341
  1377.8 69.7 %reduce-scatter.20.cloned.1.call-done = bf16[256,512]{1,0:T(8,128)(2,1)} async-done(((bf16[2048,512]{1,0:T(8,128)(2,1)}), bf16[256,512]{1,0:T(8,128)(2,1)}) %reduce-scatter.20.cloned.1.call-update) | async-done | bytes 262160 | tf_op jit(solution)/shard_map/reduce_scatter | solution.py:335
  1449.3 68.7 %reduce-scatter.26.cloned.1.call-done = bf16[256,512]{1,0:T(8,128)(2,1)} async-done(((bf16[2048,512]{1,0:T(8,128)(2,1)}), bf16[256,512]{1,0:T(8,128)(2,1)}) %reduce-scatter.26.cloned.1.call-update) | async-done | bytes 262160 | tf_op jit(solution)/shard_map/reduce_scatter | solution.py:344
  1519.7 51.3 %reduce-scatter.18.cloned.1.call-done = bf16[320,2048]{1,0:T(8,128)(2,1)} async-done(((bf16[1280,2048]{1,0:T(8,128)(2,1)}), bf16[320,2048]{1,0:T(8,128)(2,1)}) %reduce-scatter.18.cloned.1.call-update) | async-done | bytes 1310736 | tf_op jit(solution)/shard_map/reduce_scatter | solution.py:320
  1573.7 10.2 all-reduce.2
  1583.9 21.7 %all-reduce.3 = (bf16[2048]{0:T(1024)(128)(2,1)S(1)}, bf16[2048]{0:T(1024)(128)(2,1)S(1)}) all-reduce(bf16[2048]{0:T(1024)(128)(2,1)S(1)} %get-tuple-element.495, bf16[2048]{0:T(1024)(128)(2,1)S(1)} %get-tuple-element.496), channel_id=6, replica_groups=mesh['dp'=8,'tensor'=4] {'dp'}, use_global_device_ids=true, to_apply=%region_30.31.clone | all-reduce | flops 4096 | bytes 16384
  1606.3 5.8 fusion.48
  (394 shorter events, 299.2 us)
Async XLA Ops:
  7.2 103.0 %all-gather.11.cloned.1.call-start = ((), (), s32[]{:S(2)}) async-start(), calls=%async_computation.11 | async-start | bytes 6553600 | tf_op jit(solution)/shard_map/all_gather | solution.py:139
  30.1 8.8 copy-start.26
  35.2 91.5 %all-gather.13.cloned.1.call-start = ((), (), s32[]{:S(2)}) async-start(), calls=%async_computation.12 | async-start | bytes 2359296 | tf_op jit(solution)/shard_map/all_gather | solution.py:117
  36.0 179.8 %all-gather.15.cloned.1.call-start = ((), (), s32[]{:S(2)}) async-start(), calls=%async_computation.13 | async-start | bytes 2359296 | tf_op jit(solution)/shard_map/all_gather | solution.py:120
  36.7 270.8 %reduce-scatter.12.cloned.1.call-start = ((), (), s32[]{:S(2)}) async-start(), calls=%async_computation.14 | async-start | bytes 13107200 | tf_op jit(solution)/shard_map/reduce_scatter | solution.py:191
  70.4 39.8 %copy-start.9 = (bf16[2048,128]{1,0:T(8,128)(2,1)}, bf16[2048,128]{1,0:T(8,128)(2,1)S(1)}, u32[]{:S(2)}) copy-start(bf16[2048,128]{1,0:T(8,128)(2,1)S(1)} %all_gather.47) | copy-start | bytes 1572868
  108.2 28.9 %copy-start.15 = (bf16[2048,128]{1,0:T(8,128)(2,1)}, bf16[2048,128]{1,0:T(8,128)(2,1)S(1)}, u32[]{:S(2)}) copy-start(bf16[2048,128]{1,0:T(8,128)(2,1)S(1)} %all_gather.48) | copy-start | bytes 1572868
  110.2 23.0 %copy-start.11 = (f32[1280,64]{0,1:T(8,128)}, f32[1280,64]{0,1:T(8,128)S(1)}, u32[]{:S(2)}) copy-start(f32[1280,64]{0,1:T(8,128)S(1)} %get-tuple-element.525) | copy-start | bytes 983044
  215.8 7.7 copy-start.19
  223.5 18.8 %copy-start.35 = (s32[320]{0:T(512)S(1)}, s32[320]{0:T(512)}, u32[]{:S(2)}) copy-start(s32[320]{0:T(512)} %param.22) | copy-start | bytes 3844
  223.5 276.3 %all-gather.19.cloned.1.call-start = ((), (), s32[]{:S(2)}) async-start(), calls=%async_computation.16 | async-start | bytes 6488064 | tf_op jit(solution)/shard_map/all_gather | solution.py:126
  224.1 302.4 %all-gather.17.cloned.1.call-start = ((), (), s32[]{:S(2)}) async-start(), calls=%async_computation.15 | async-start | bytes 6553600 | tf_op jit(solution)/shard_map/all_gather | solution.py:202
  242.3 617.1 %copy-start.22 = (f32[8,1,256]{2,1,0:T(1,128)}, f32[8,1,256]{2,1,0:T(1,128)S(1)}, u32[]{:S(2)}) copy-start(f32[8,1,256]{2,1,0:T(1,128)S(1)} %convert_element_type.220) | copy-start | bytes 24580
  311.9 547.6 %copy-start.1 = (f32[320,2048]{1,0:T(8,128)}, f32[320,2048]{1,0:T(8,128)S(1)}, u32[]{:S(2)}) copy-start(f32[320,2048]{1,0:T(8,128)S(1)} %get-tuple-element.500) | copy-start | bytes 7864324
  311.9 547.6 %copy-start.28 = (f32[320]{0:T(512)}, f32[320]{0:T(512)S(1)}, u32[]{:S(2)}) copy-start(f32[320]{0:T(512)S(1)} %add_rsqrt_fusion) | copy-start | bytes 3844
  313.3 308.1 %all-gather.21.cloned.1.call-start = ((), (), s32[]{:S(2)}) async-start(), calls=%async_computation.17 | async-start | bytes 6488064 | tf_op jit(solution)/shard_map/all_gather | solution.py:128
  314.0 348.1 %all-gather.23.cloned.1.call-start = ((), (), s32[]{:S(2)}) async-start(), calls=%async_computation.19 | async-start | bytes 6553600 | tf_op jit(solution)/shard_map/all_gather | solution.py:220
  314.1 33.0 %collective-permute-start = (bf16[256,1408]{1,0:T(8,128)(2,1)S(1)}, bf16[256,1408]{1,0:T(8,128)(2,1)}, u32[]{:S(2)}, u32[]{:S(2)}) collective-permute-start(bf16[256,1408]{1,0:T(8,128)(2,1)S(1)} %copy-done.21), channel_id=1, source_target_pairs={{0,4},{4,8},{8,12},{12,16},{16,20},{20,24},{24,28},{28,0},{1,5},{5... | collective-permute-start | bytes 2162696 | tf_op jit(solution)/shard_map/ppermute | solution.py:25
  347.1 42.5 %collective-permute-start.1 = (bf16[256,1408]{1,0:T(8,128)(2,1)}, bf16[256,1408]{1,0:T(8,128)(2,1)}, u32[]{:S(2)}, u32[]{:S(2)}) collective-permute-start(bf16[256,1408]{1,0:T(8,128)(2,1)} %collective-permute-done), channel_id=1, source_target_pairs={{0,4},{4,8},{8,12},{12,16},{16,20},{20,24},{24,28},{28,0},{1,5},{5... | collective-permute-start | bytes 2162696 | tf_op jit(solution)/shard_map/ppermute | solution.py:25
  347.1 458.5 %reduce-scatter.16.cloned.1.call-start = ((), (), s32[]{:S(2)}) async-start(), calls=%async_computation.20 | async-start | bytes 13107200 | tf_op jit(solution)/shard_map/reduce_scatter | solution.py:233
  347.1 44.9 %collective-permute-start.4 = (bf16[256,1408]{1,0:T(8,128)(2,1)S(1)}, bf16[256,1408]{1,0:T(8,128)(2,1)}, u32[]{:S(2)}, u32[]{:S(2)}) collective-permute-start(bf16[256,1408]{1,0:T(8,128)(2,1)S(1)} %copy-done.21), channel_id=1, source_target_pairs={{4,0},{8,4},{12,8},{16,12},{20,16},{24,20},{28,24},{0,28},{5,1},{9... | collective-permute-start | bytes 2162696 | tf_op jit(solution)/shard_map/ppermute | solution.py:27
  389.6 48.5 %collective-permute-start.2 = (bf16[256,1408]{1,0:T(8,128)(2,1)}, bf16[256,1408]{1,0:T(8,128)(2,1)}, u32[]{:S(2)}, u32[]{:S(2)}) collective-permute-start(bf16[256,1408]{1,0:T(8,128)(2,1)} %collective-permute-done.1), channel_id=1, source_target_pairs={{0,4},{4,8},{8,12},{12,16},{16,20},{20,24},{24,28},{28,0},{1,5},{5... | collective-permute-start | bytes 2162696 | tf_op jit(solution)/shard_map/ppermute | solution.py:25
  392.1 51.2 %collective-permute-start.5 = (bf16[256,1408]{1,0:T(8,128)(2,1)}, bf16[256,1408]{1,0:T(8,128)(2,1)}, u32[]{:S(2)}, u32[]{:S(2)}) collective-permute-start(bf16[256,1408]{1,0:T(8,128)(2,1)} %collective-permute-done.4), channel_id=1, source_target_pairs={{4,0},{8,4},{12,8},{16,12},{20,16},{24,20},{28,24},{0,28},{5,1},{9... | collective-permute-start | bytes 2162696 | tf_op jit(solution)/shard_map/ppermute | solution.py:27
  438.1 40.5 %collective-permute-start.3 = (bf16[256,1408]{1,0:T(8,128)(2,1)}, bf16[256,1408]{1,0:T(8,128)(2,1)}, u32[]{:S(2)}, u32[]{:S(2)}) collective-permute-start(bf16[256,1408]{1,0:T(8,128)(2,1)} %collective-permute-done.2), channel_id=1, source_target_pairs={{0,4},{4,8},{8,12},{12,16},{16,20},{20,24},{24,28},{28,0},{1,5},{5... | collective-permute-start | bytes 2162696 | tf_op jit(solution)/shard_map/ppermute | solution.py:25
  443.3 48.4 %collective-permute-start.6 = (bf16[256,1408]{1,0:T(8,128)(2,1)}, bf16[256,1408]{1,0:T(8,128)(2,1)S(1)}, u32[]{:S(2)}, u32[]{:S(2)}) collective-permute-start(bf16[256,1408]{1,0:T(8,128)(2,1)} %collective-permute-done.5), channel_id=1, source_target_pairs={{4,0},{8,4},{12,8},{16,12},{20,16},{24,20},{28,24},{0,28},{5,1},{9... | collective-permute-start | bytes 2162696 | tf_op jit(solution)/shard_map/ppermute | solution.py:27
  662.1 13.9 copy-start.36
  662.1 44.8 %slice-start = ((s8[5767168]{0:T(1024)(128)(4,1)}), s8[4194304]{0:T(1024)(128)(4,1)S(1)}, s32[]{:S(2)}) async-start(s8[5767168]{0:T(1024)(128)(4,1)} %bitcast.224), calls=%async_computation.30 | async-start | bytes 8388608
  676.0 31.0 %slice-start.1 = ((s8[5767168]{0:T(1024)(128)(4,1)}), s8[1572864]{0:T(1024)(128)(4,1)S(1)}, s32[]{:S(2)}) async-start(s8[5767168]{0:T(1024)(128)(4,1)} %bitcast.224), calls=%async_computation.31 | async-start | bytes 3145728
  692.9 14.0 copy-start.42
  720.1 139.3 %reduce-scatter.14.cloned.1.call-start = ((), (), s32[]{:S(2)}) async-start(), calls=%async_computation.18 | async-start | bytes 6553600 | tf_op jit(solution)/shard_map/reduce_scatter | solution.py:208
  733.5 174.1 %all-gather.25.cloned.1.call-start = ((), (), s32[]{:S(2)}) async-start(), calls=%async_computation.21 | async-start | bytes 6553600 | tf_op jit(solution)/shard_map/all_gather | solution.py:257
  808.6 55.9 %copy-start.33 = (f32[320]{0:T(512)}, f32[320]{0:T(512)S(1)}, u32[]{:S(2)}) copy-start(f32[320]{0:T(512)S(1)} %broadcast_multiply_fusion.1) | copy-start | bytes 3844
  864.6 256.5 %reduce-scatter.28.cloned.1.call-start = ((), (), s32[]{:S(2)}) async-start(), calls=%async_computation.27 | async-start | bytes 6488064 | tf_op jit(solution)/shard_map/reduce_scatter | solution.py:245
  877.6 255.4 %reduce-scatter.30.cloned.1.call-start = ((), (), s32[]{:S(2)}) async-start(), calls=%async_computation.28 | async-start | bytes 6488064 | tf_op jit(solution)/shard_map/reduce_scatter | solution.py:248
  891.2 355.5 %reduce-scatter.32.cloned.1.call-start = ((), (), s32[]{:S(2)}) async-start(), calls=%async_computation.29 | async-start | bytes 6488064 | tf_op jit(solution)/shard_map/reduce_scatter | solution.py:251
  907.6 404.6 %reduce-scatter.22.cloned.1.call-start = ((), (), s32[]{:S(2)}) async-start(), calls=%async_computation.24 | async-start | bytes 589824 | tf_op jit(solution)/shard_map/reduce_scatter | solution.py:338
  1076.1 300.2 %reduce-scatter.24.cloned.1.call-start = ((), (), s32[]{:S(2)}) async-start(), calls=%async_computation.25 | async-start | bytes 589824 | tf_op jit(solution)/shard_map/reduce_scatter | solution.py:341
  1084.6 362.9 %reduce-scatter.20.cloned.1.call-start = ((), (), s32[]{:S(2)}) async-start(), calls=%async_computation.23 | async-start | bytes 2359296 | tf_op jit(solution)/shard_map/reduce_scatter | solution.py:335
  1096.4 7.2 copy-start.10
  1096.4 421.5 %reduce-scatter.26.cloned.1.call-start = ((), (), s32[]{:S(2)}) async-start(), calls=%async_computation.26 | async-start | bytes 2359296 | tf_op jit(solution)/shard_map/reduce_scatter | solution.py:344
  1103.6 467.4 %reduce-scatter.18.cloned.1.call-start = ((), (), s32[]{:S(2)}) async-start(), calls=%async_computation.22 | async-start | bytes 6553600 | tf_op jit(solution)/shard_map/reduce_scatter | solution.py:320
  1123.4 447.6 %copy-start.25 = (f32[8,1,256]{2,1,0:T(1,128)S(1)}, f32[8,1,256]{2,1,0:T(1,128)}, u32[]{:S(2)}) copy-start(f32[8,1,256]{2,1,0:T(1,128)} %copy-done.24) | copy-start | bytes 24580
  1123.4 447.6 %copy-start.32 = (f32[320]{0:T(512)S(1)}, f32[320]{0:T(512)}, u32[]{:S(2)}) copy-start(f32[320]{0:T(512)} %copy-done.31) | copy-start | bytes 3844
  1249.1 324.6 %copy-start.30 = (f32[2048]{0:T(1024)S(1)}, f32[2048]{0:T(1024)}, u32[]{:S(2)}) copy-start(f32[2048]{0:T(1024)} %get-tuple-element.453) | copy-start | bytes 24580
  1249.1 357.2 %copy-start.2 = (f32[320,2048]{1,0:T(8,128)S(1)}, f32[320,2048]{1,0:T(8,128)}, u32[]{:S(2)}) copy-start(f32[320,2048]{1,0:T(8,128)} %copy-done.1) | copy-start | bytes 7864324
  1249.1 357.2 %copy-start.23 = (f32[8,1,256]{2,1,0:T(1,128)S(1)}, f32[8,1,256]{2,1,0:T(1,128)}, u32[]{:S(2)}) copy-start(f32[8,1,256]{2,1,0:T(1,128)} %copy-done.22) | copy-start | bytes 24580
  1249.1 357.2 %copy-start.29 = (f32[320]{0:T(512)S(1)}, f32[320]{0:T(512)}, u32[]{:S(2)}) copy-start(f32[320]{0:T(512)} %copy-done.28) | copy-start | bytes 3844
  1249.1 357.2 %copy-start.34 = (f32[320]{0:T(512)S(1)}, f32[320]{0:T(512)}, u32[]{:S(2)}) copy-start(f32[320]{0:T(512)} %copy-done.33) | copy-start | bytes 3844
  (44 other events, 109.7 us)
Sparse Core Ops, SparseCore 0:
  35.3 37.8 all-gather.10
  75.4 51.2 all-gather.12
  128.8 47.7 all-gather.14
  223.6 83.8 reduce-scatter.11
  309.5 169.1 all-gather.18
  480.7 45.7 all-gather.16
  528.6 92.6 all-gather.20
  623.5 38.6 all-gather.22
  720.3 85.2 reduce-scatter.15
  808.0 51.3 reduce-scatter.13
  864.7 40.4 all-gather.24
  909.1 109.9 reduce-scatter.27
  1023.2 109.7 reduce-scatter.29
  1137.0 109.7 reduce-scatter.31
  1250.3 61.7 reduce-scatter.21
  1315.3 60.9 reduce-scatter.23
  1380.6 66.7 reduce-scatter.19
  1451.3 66.6 reduce-scatter.25
  1520.6 50.3 reduce-scatter.17
